TPU v7x, 32 devices: a whole 2x2x4 slice. The times are simulated.
32 devices in a mesh: img: 8 (over z, x), seq: 4 (over y, core).
Axes of the slice: x: 2, y: 2, z: 4, core: 2. Of those that a mesh axis runs over, the one named last changes fastest.
Arguments:
- patches: bfloat16 [16, 1024, 1024], P('img', 'seq'), may hold values from -6 to 6
- cotangent: bfloat16 [16, 1024, 1024], P('img', 'seq'), may hold values from -6 to 6
- res_ids: int32 [16, 20], P('img'), may hold values from 0 to 384, as said below
- pos_table: float32 [49, 1024], replicated, may hold values from -3 to 3
- attn_in: float32 [1024, 3072], P(('img', 'seq')), may hold values from -0.1875 to 0.1875
- attn_out: float32 [1024, 1024], P(('img', 'seq')), may hold values from -0.5 to 0.5
- mlp_in: float32 [1024, 4096], P(('img', 'seq')), may hold values from -0.1875 to 0.1875
- mlp_out: float32 [4096, 1024], P(('img', 'seq')), may hold values from -0.09375 to 0.09375
- vectors: float32 [1024, 12], P(('img', 'seq')), may hold values from -1 to 1.75
- first_attn_in: float32 [1024, 3072], P(('img', 'seq')), may hold values from -0.0018 to 0.0018
- first_attn_out: float32 [1024, 1024], P(('img', 'seq')), may hold values from -0.0018 to 0.0018
- first_mlp_in: float32 [1024, 4096], P(('img', 'seq')), may hold values from -0.0018 to 0.0018
- first_mlp_out: float32 [4096, 1024], P(('img', 'seq')), may hold values from -0.0018 to 0.0018
- first_vectors: float32 [1024, 12], P(('img', 'seq')), may hold values from -0.0018 to 0.0018
- second_attn_in: float32 [1024, 3072], P(('img', 'seq')), may hold values from 3e-09 to 3e-07
- second_attn_out: float32 [1024, 1024], P(('img', 'seq')), may hold values from 3e-09 to 3e-07
- second_mlp_in: float32 [1024, 4096], P(('img', 'seq')), may hold values from 3e-09 to 3e-07
- second_mlp_out: float32 [4096, 1024], P(('img', 'seq')), may hold values from 3e-09 to 3e-07
- second_vectors: float32 [1024, 12], P(('img', 'seq')), may hold values from 3e-09 to 3e-07
Outputs:
- output: bfloat16 [16, 1024, 1024], P('img', 'seq')
- input_grad: bfloat16 [16, 1024, 1024], P('img', 'seq')
- table_grad: float32 [49, 1024], replicated
- grad_attn_in: float32 [1024, 3072], P(('img', 'seq'))
- grad_attn_out: float32 [1024, 1024], P(('img', 'seq'))
- grad_mlp_in: float32 [1024, 4096], P(('img', 'seq'))
- grad_mlp_out: float32 [4096, 1024], P(('img', 'seq'))
- grad_vectors: float32 [1024, 12], P(('img', 'seq'))
- update_attn_in: float32 [1024, 3072], P(('img', 'seq'))
- update_attn_out: float32 [1024, 1024], P(('img', 'seq'))
- update_mlp_in: float32 [1024, 4096], P(('img', 'seq'))
- update_mlp_out: float32 [4096, 1024], P(('img', 'seq'))
- update_vectors: float32 [1024, 12], P(('img', 'seq'))
- new_first_attn_in: float32 [1024, 3072], P(('img', 'seq'))
- new_first_attn_out: float32 [1024, 1024], P(('img', 'seq'))
- new_first_mlp_in: float32 [1024, 4096], P(('img', 'seq'))
- new_first_mlp_out: float32 [4096, 1024], P(('img', 'seq'))
- new_first_vectors: float32 [1024, 12], P(('img', 'seq'))
- new_second_attn_in: float32 [1024, 3072], P(('img', 'seq'))
- new_second_attn_out: float32 [1024, 1024], P(('img', 'seq'))
- new_second_mlp_in: float32 [1024, 4096], P(('img', 'seq'))
- new_second_mlp_out: float32 [4096, 1024], P(('img', 'seq'))
- new_second_vectors: float32 [1024, 12], P(('img', 'seq'))
Inputs may be any that keep to these rules, and one draw needn't show every extreme that they name: `res_ids`: each entry is 224, 384 or 0; a 0 is followed only by 0s in its row; a row's images fit within its 1024 tokens.
All inputs are finite; a program needn't handle non-finite values.
Results may differ from a plain program's by a relative error of at most 0.018.
Values may be sent and summed in bfloat16 or wider, within the bound.
No kernel may reach another device: no remote copies, remote signals or barrier semaphores. Data moves between devices by JAX's collectives and lax.ppermute only.
A program may use at most 256 MiB of HBM per device.

v0:
```python
import jax
import jax.numpy as jnp
from jax import lax
from jax.sharding import PartitionSpec as P

HEADS = 16
GRID = 7
GRID_HI = 12
PRECISE = lax.Precision.HIGHEST
FIRST_CORRECTION = 0.9999734386011124
SECOND_CORRECTION = 0.0952078528862911


def layout(res_ids, positions):
    grid_side = jnp.where(res_ids == 384, GRID_HI, jnp.where(res_ids == 224, GRID, 0)).astype(
        jnp.int32
    )
    lengths = grid_side * grid_side
    starts = jnp.cumsum(lengths, axis=1) - lengths
    places = positions[None, :, None]
    inside = ((places >= starts[:, None, :]) & (places < (starts + lengths)[:, None, :])).astype(
        jnp.int32
    )
    image_number = jnp.arange(res_ids.shape[1], dtype=jnp.int32)
    usable = jnp.sum(inside, axis=2)
    segment = jnp.sum(inside * image_number, axis=2) + (1 - usable) * res_ids.shape[1]
    start_of = jnp.sum(inside * starts[:, None, :], axis=2)
    side_of = jnp.sum(inside * grid_side[:, None, :], axis=2)
    patch_index = (positions[None, :] - start_of) * usable
    return (segment, side_of, patch_index, usable)


def axis_weights(coord, side_of):
    scaled = jnp.maximum((2 * coord + 1) * GRID - GRID_HI, 0)
    lower_fine = scaled // (2 * GRID_HI)
    fraction_fine = (scaled - lower_fine * 2 * GRID_HI).astype(jnp.float32) / (2.0 * GRID_HI)
    resized = side_of == GRID_HI
    lower_cell = jnp.where(resized, lower_fine, coord)
    fraction = jnp.where(resized, fraction_fine, jnp.zeros_like(fraction_fine))
    upper_cell = jnp.minimum(lower_cell + 1, GRID - 1)
    cell_index = jnp.arange(GRID, dtype=jnp.int32)
    below = (cell_index == lower_cell[..., None]).astype(jnp.float32)
    above = (cell_index == upper_cell[..., None]).astype(jnp.float32)
    return (1.0 - fraction)[..., None] * below + fraction[..., None] * above


def table_weights(side_of, patch_index, usable):
    safe_side = jnp.maximum(side_of, 1)
    row_coord = patch_index // safe_side
    column_coord = patch_index % safe_side
    outer = (
        axis_weights(row_coord, side_of)[..., :, None]
        * axis_weights(column_coord, side_of)[..., None, :]
    )
    outer = outer * usable.astype(jnp.float32)[..., None, None]
    return outer.reshape(side_of.shape + (GRID * GRID,))


def layer_norm(stream, gain, shift):
    center = jnp.mean(stream, axis=-1, keepdims=True)
    centered = stream - center
    spread = jnp.mean(centered * centered, axis=-1, keepdims=True)
    return centered * lax.rsqrt(spread + 1e-06) * gain + shift


def gelu_exact(values):
    return jax.nn.gelu(values, approximate=False)


def by_transpose(left, right):
    return lax.dot_general(
        left, right, (((1,), (1,)), ((), ())), preferred_element_type=jnp.float32
    )


def transpose_by(left, right):
    return lax.dot_general(
        left, right, (((0,), (0,)), ((), ())), preferred_element_type=jnp.float32
    )


def adam_update(weight, gradient, first_moment, second_moment, factor, decay):
    scaled = gradient * factor
    first_new = 0.9 * first_moment + 0.1 * scaled
    second_new = 0.999 * second_moment + 0.001 * scaled * scaled
    first_hat = first_new / FIRST_CORRECTION
    second_hat = second_new / SECOND_CORRECTION
    direction = first_hat / (jnp.sqrt(second_hat) + 1e-08) + decay * weight
    return (direction, first_new, second_new)


def masked_scores(query_heads, key_heads, allowed, score_scale):
    scores = (
        jnp.einsum("rqhe,rkhe->rhqk", query_heads, key_heads, preferred_element_type=jnp.float32)
        * score_scale
    )
    return jnp.where(allowed[:, None], scores, -1e30)


def per_device(
    patches,
    cotangent,
    res_ids,
    pos_table,
    attn_in,
    attn_out,
    mlp_in,
    mlp_out,
    vectors,
    first_attn_in,
    first_attn_out,
    first_mlp_in,
    first_mlp_out,
    first_vectors,
    second_attn_in,
    second_attn_out,
    second_mlp_in,
    second_mlp_out,
    second_vectors,
):
    row_count, local_len, model_width = patches.shape
    seq_count = lax.axis_size("seq")
    row_len = local_len * seq_count
    token_count = row_count * local_len
    head_count = HEADS
    head_size = model_width // head_count
    score_scale = head_size ** (-0.5)
    slot_total = row_count * lax.axis_size("img") * row_len
    all_positions = jnp.arange(row_len, dtype=jnp.int32)
    segment_all, side_all, patch_all, usable_all = layout(res_ids, all_positions)
    offset = lax.axis_index("seq") * local_len

    def local_part(array):
        return lax.dynamic_slice_in_dim(array, offset, local_len, 1)

    segment = local_part(segment_all)
    usable = local_part(usable_all)
    place = table_weights(local_part(side_all), local_part(patch_all), usable).reshape(
        token_count, GRID * GRID
    )
    usable_float = usable.reshape(token_count).astype(jnp.float32)[:, None]
    cast_in = attn_in.astype(jnp.bfloat16)
    cast_out = attn_out.astype(jnp.bfloat16)
    cast_up = mlp_in.astype(jnp.bfloat16)
    cast_down = mlp_out.astype(jnp.bfloat16)
    cast_vectors = vectors.astype(jnp.bfloat16)
    gathered = (
        lax.all_gather(cast_in, ("img", "seq"), axis=0, tiled=True),
        lax.all_gather(cast_out, ("img", "seq"), axis=0, tiled=True),
        lax.all_gather(cast_up, ("img", "seq"), axis=0, tiled=True),
        lax.all_gather(cast_down, ("img", "seq"), axis=0, tiled=True),
        lax.all_gather(cast_vectors, ("img", "seq"), axis=0, tiled=True),
    )
    in_matrix, out_matrix, up_matrix, down_matrix, vector_low = gathered
    vector_cols = vector_low.astype(jnp.float32)
    stream = patches.reshape(token_count, model_width).astype(jnp.float32) + jnp.dot(
        place, pos_table, precision=PRECISE, preferred_element_type=jnp.float32
    )
    normed_one = layer_norm(stream, vector_cols[:, 0], vector_cols[:, 1]).astype(jnp.bfloat16)
    projected = jnp.dot(normed_one, in_matrix, preferred_element_type=jnp.float32)
    query = (projected[:, :model_width] + vector_cols[:, 2]).astype(jnp.bfloat16)
    key_rows = (
        projected[:, model_width : 2 * model_width]
        .astype(jnp.bfloat16)
        .reshape(row_count, local_len, model_width)
    )
    value_rows = (
        (projected[:, 2 * model_width :] + vector_cols[:, 3])
        .astype(jnp.bfloat16)
        .reshape(row_count, local_len, model_width)
    )
    keys_all, values_all = (
        lax.all_gather(key_rows, "seq", axis=1, tiled=True),
        lax.all_gather(value_rows, "seq", axis=1, tiled=True),
    )
    key_len = keys_all.shape[1]
    query_heads = query.reshape(row_count, local_len, head_count, head_size)
    key_heads = keys_all.reshape(row_count, key_len, head_count, head_size)
    value_heads = values_all.reshape(row_count, key_len, head_count, head_size)
    allowed = segment[:, :, None] == segment_all[:, None, :]
    scores = masked_scores(query_heads, key_heads, allowed, score_scale)
    highest = jnp.max(scores, axis=-1, keepdims=True)
    exponent = jnp.exp(scores - highest)
    totals = jnp.sum(exponent, axis=-1, keepdims=True)
    probs = exponent / totals
    log_total = highest + jnp.log(totals)
    mixed = jnp.einsum(
        "rhqk,rkhe->rqhe",
        probs.astype(jnp.bfloat16),
        value_heads,
        preferred_element_type=jnp.float32,
    )
    attended = mixed.reshape(token_count, model_width).astype(jnp.bfloat16)
    branch = jnp.dot(attended, out_matrix, preferred_element_type=jnp.float32) + vector_cols[:, 4]
    stream_two = stream + branch
    normed_two = layer_norm(stream_two, vector_cols[:, 5], vector_cols[:, 6]).astype(jnp.bfloat16)
    hidden_pre = jnp.dot(normed_two, up_matrix, preferred_element_type=jnp.float32) + vector_cols[
        :, 8:
    ].reshape(-1)
    hidden = gelu_exact(hidden_pre).astype(jnp.bfloat16)
    last = jnp.dot(hidden, down_matrix, preferred_element_type=jnp.float32) + vector_cols[:, 7]
    output = (
        ((stream_two + last) * usable_float)
        .reshape(row_count, local_len, model_width)
        .astype(jnp.bfloat16)
    )
    grad_out_rows = cotangent.reshape(token_count, model_width).astype(jnp.float32) * usable_float
    grad_out_low = grad_out_rows.astype(jnp.bfloat16)
    grad_bias_down = jnp.sum(grad_out_low.astype(jnp.float32), axis=0)
    grad_down = transpose_by(hidden, grad_out_low)
    grad_hidden = by_transpose(grad_out_low, down_matrix)
    grad_pre = jax.vjp(gelu_exact, hidden_pre)[1](grad_hidden)[0]
    grad_pre_low = grad_pre.astype(jnp.bfloat16)
    grad_bias_up = jnp.sum(grad_pre_low.astype(jnp.float32), axis=0)
    grad_up = transpose_by(normed_two, grad_pre_low)
    grad_normed_two = by_transpose(grad_pre_low, up_matrix)
    norm_two_pull = jax.vjp(layer_norm, stream_two, vector_cols[:, 5], vector_cols[:, 6])[1]
    grad_stream_norm, grad_gain_two, grad_shift_two = norm_two_pull(grad_normed_two)
    grad_stream_two = grad_out_rows + grad_stream_norm
    grad_branch_low = grad_stream_two.astype(jnp.bfloat16)
    grad_bias_out = jnp.sum(grad_branch_low.astype(jnp.float32), axis=0)
    grad_out_matrix = transpose_by(attended, grad_branch_low)
    grad_mixed = by_transpose(grad_branch_low, out_matrix).astype(jnp.bfloat16)
    grad_mixed_heads = grad_mixed.reshape(row_count, local_len, head_count, head_size)
    scores_again = masked_scores(query_heads, key_heads, allowed, score_scale)
    probs_again = jnp.exp(scores_again - log_total)
    value_part = jnp.einsum(
        "rhqk,rqhe->rkhe",
        probs_again.astype(jnp.bfloat16),
        grad_mixed_heads,
        preferred_element_type=jnp.float32,
    )
    grad_probs = jnp.einsum(
        "rqhe,rkhe->rhqk", grad_mixed_heads, value_heads, preferred_element_type=jnp.float32
    )
    inner_sum = jnp.sum(grad_probs * probs_again, axis=-1, keepdims=True)
    grad_scores = (probs_again * (grad_probs - inner_sum)).astype(jnp.bfloat16)
    grad_query = (
        jnp.einsum("rhqk,rkhe->rqhe", grad_scores, key_heads, preferred_element_type=jnp.float32)
        * score_scale
    )
    key_part = (
        jnp.einsum("rhqk,rqhe->rkhe", grad_scores, query_heads, preferred_element_type=jnp.float32)
        * score_scale
    )
    key_part = key_part.reshape(row_count, key_len, model_width)
    value_part = value_part.reshape(row_count, key_len, model_width)
    grad_keys, grad_values = (
        lax.psum_scatter(
            key_part.astype(jnp.bfloat16), "seq", scatter_dimension=1, tiled=True
        ).astype(jnp.float32),
        lax.psum_scatter(
            value_part.astype(jnp.bfloat16), "seq", scatter_dimension=1, tiled=True
        ).astype(jnp.float32),
    )
    grad_query_low = grad_query.reshape(token_count, model_width).astype(jnp.bfloat16)
    grad_keys_low = grad_keys.reshape(token_count, model_width).astype(jnp.bfloat16)
    grad_values_low = grad_values.reshape(token_count, model_width).astype(jnp.bfloat16)
    grad_projected = jnp.concatenate([grad_query_low, grad_keys_low, grad_values_low], axis=1)
    grad_in_matrix = transpose_by(normed_one, grad_projected)
    grad_bias_query = jnp.sum(grad_query_low.astype(jnp.float32), axis=0)
    grad_bias_value = jnp.sum(grad_values_low.astype(jnp.float32), axis=0)
    grad_normed_one = by_transpose(grad_projected, in_matrix)
    norm_one_pull = jax.vjp(layer_norm, stream, vector_cols[:, 0], vector_cols[:, 1])[1]
    grad_stream_first, grad_gain_one, grad_shift_one = norm_one_pull(grad_normed_one)
    grad_stream = grad_stream_two + grad_stream_first
    input_grad = grad_stream.reshape(row_count, local_len, model_width).astype(jnp.bfloat16)
    table_part = lax.dot_general(
        place,
        grad_stream,
        (((0,), (0,)), ((), ())),
        precision=PRECISE,
        preferred_element_type=jnp.float32,
    )
    table_grad = lax.psum(table_part, ("img", "seq"))
    grad_vector_cols = jnp.concatenate(
        [
            jnp.stack(
                [
                    grad_gain_one,
                    grad_shift_one,
                    grad_bias_query,
                    grad_bias_value,
                    grad_bias_out,
                    grad_gain_two,
                    grad_shift_two,
                    grad_bias_down,
                ],
                axis=1,
            ),
            grad_bias_up.reshape(model_width, -1),
        ],
        axis=1,
    )
    shards = (
        lax.psum_scatter(grad_in_matrix, ("img", "seq"), scatter_dimension=0, tiled=True),
        lax.psum_scatter(grad_out_matrix, ("img", "seq"), scatter_dimension=0, tiled=True),
        lax.psum_scatter(grad_up, ("img", "seq"), scatter_dimension=0, tiled=True),
        lax.psum_scatter(grad_down, ("img", "seq"), scatter_dimension=0, tiled=True),
        lax.psum_scatter(grad_vector_cols, ("img", "seq"), scatter_dimension=0, tiled=True),
    )
    factor = jnp.float32(1.0 / slot_total)
    weights = (attn_in, attn_out, mlp_in, mlp_out, vectors)
    firsts = (first_attn_in, first_attn_out, first_mlp_in, first_mlp_out, first_vectors)
    seconds = (second_attn_in, second_attn_out, second_mlp_in, second_mlp_out, second_vectors)
    decays = (0.05, 0.05, 0.05, 0.05, 0.0)
    updated = [
        adam_update(
            weights[index], shards[index], firsts[index], seconds[index], factor, decays[index]
        )
        for index in range(5)
    ]
    return (
        output,
        input_grad,
        table_grad,
        shards[0],
        shards[1],
        shards[2],
        shards[3],
        shards[4],
        updated[0][0],
        updated[1][0],
        updated[2][0],
        updated[3][0],
        updated[4][0],
        updated[0][1],
        updated[1][1],
        updated[2][1],
        updated[3][1],
        updated[4][1],
        updated[0][2],
        updated[1][2],
        updated[2][2],
        updated[3][2],
        updated[4][2],
    )


def solution(mesh):
    return jax.shard_map(
        per_device,
        mesh=mesh,
        in_specs=(
            P("img", "seq", None),
            P("img", "seq", None),
            P("img", None),
            P(),
            P(("img", "seq"), None),
            P(("img", "seq"), None),
            P(("img", "seq"), None),
            P(("img", "seq"), None),
            P(("img", "seq"), None),
            P(("img", "seq"), None),
            P(("img", "seq"), None),
            P(("img", "seq"), None),
            P(("img", "seq"), None),
            P(("img", "seq"), None),
            P(("img", "seq"), None),
            P(("img", "seq"), None),
            P(("img", "seq"), None),
            P(("img", "seq"), None),
            P(("img", "seq"), None),
        ),
        out_specs=(
            P("img", "seq", None),
            P("img", "seq", None),
            P(),
            P(("img", "seq"), None),
            P(("img", "seq"), None),
            P(("img", "seq"), None),
            P(("img", "seq"), None),
            P(("img", "seq"), None),
            P(("img", "seq"), None),
            P(("img", "seq"), None),
            P(("img", "seq"), None),
            P(("img", "seq"), None),
            P(("img", "seq"), None),
            P(("img", "seq"), None),
            P(("img", "seq"), None),
            P(("img", "seq"), None),
            P(("img", "seq"), None),
            P(("img", "seq"), None),
            P(("img", "seq"), None),
            P(("img", "seq"), None),
            P(("img", "seq"), None),
            P(("img", "seq"), None),
            P(("img", "seq"), None),
        ),
        check_vma=False,
    )
```

profile of v0, /device:TPU:1, one launch (start us, length us, event | category | flops | bytes accessed | tf_op | source)
XLA Modules:
  0.0 1508.1 jit_solution(4276140562138739996)
XLA Ops:
  12.7 43.8 %all-gather = bf16[32,32,12]{1,2,0:T(8,128)(2,1)S(1)} all-gather(bf16[1,32,12]{1,2,0:T(8,128)(2,1)S(1)} %convert_bitcast_fusion), channel_id=1, replica_groups=mesh['img'=8,'seq'=4] {'img','seq'}, dimensions={0}, use_global_device_ids=true | all-gather | bytes 25344 | tf_op jit(solution)/shard_map/all_gather | solution.py:152
  61.2 22.5 %all-gather.8.cloned.1.call-done = bf16[1024,3072]{1,0:T(8,128)(2,1)} async-done(((bf16[32,3072]{1,0:T(8,128)(2,1)}), bf16[1024,3072]{1,0:T(8,128)(2,1)}) %all-gather.8.cloned.1.call-update) | async-done | bytes 6291472 | tf_op jit(solution)/shard_map/all_gather | solution.py:148
  114.5 12.0 all-gather.12.cloned.1.call-done
  126.5 6.2 copy.162
  132.7 30.4 %all-gather.10.cloned.1.call-done = bf16[2,1024,1024]{2,1,0:T(8,128)(2,1)} async-done(((bf16[2,256,1024]{2,1,0:T(8,128)(2,1)}), bf16[2,1024,1024]{2,1,0:T(8,128)(2,1)}) %all-gather.10.cloned.1.call-update) | async-done | bytes 4194320 | tf_op jit(solution)/shard_map/all_gather | solution.py:174
  169.3 16.1 %fusion.46 = (f32[2,16,256]{2,1,0:T(8,128)S(1)}, f32[2,16,256,1024]{3,2,1,0:T(8,128)}) fusion(bf16[2,256,16,64]{1,3,2,0:T(8,128)(2,1)S(1)} %copy.163, bf16[2,1024,16,64]{1,3,2,0:T(8,128)(2,1)} %bitcast.100, pred[2,256,1024]{2,1,0:T(8,128)(4,1)} %broadcast_compare_fusion), kind=kOutput, calls=%fused_computation.146 | convolution fusion | flops 1098899456 | bytes 39354368 | tf_op jit(solution)/shard_map/rqhe,rkhe->rhqk/dot_general | solution.py:94
  185.4 14.4 fusion
  199.8 15.5 %fusion.19 = bf16[2,256,16,64]{1,3,2,0:T(8,128)(2,1)S(1)} fusion(bf16[2,1024,16,64]{1,3,2,0:T(8,128)(2,1)} %bitcast.102, f32[2,16,256,1024]{3,2,1,0:T(8,128)} %get-tuple-element.135, f32[2,16,256]{2,1,0:T(8,128)S(1)} %fusion, f32[2,16,256]{2,1,0:T(8,128)S(1)} %get-tuple-element.134), kind=kOutput, calls=%fused_computation.62 | convolution fusion | flops 1099431936 | bytes 38862848 | tf_op jit(solution)/shard_map/rhqk,rkhe->rqhe/dot_general | solution.py:187
  216.6 6.3 all-gather.14.cloned.1.call-done
  227.6 75.0 %all-gather.16.cloned.1.call-done = bf16[1024,4096]{1,0:T(8,128)(2,1)} async-done(((bf16[32,4096]{1,0:T(8,128)(2,1)}), bf16[1024,4096]{1,0:T(8,128)(2,1)}) %all-gather.16.cloned.1.call-update) | async-done | bytes 8388624 | tf_op jit(solution)/shard_map/all_gather | solution.py:150
  302.6 12.0 fusion.38
  314.6 67.4 %all-gather.18.cloned.1.call-done = bf16[4096,1024]{1,0:T(8,128)(2,1)} async-done(((bf16[128,1024]{1,0:T(8,128)(2,1)}), bf16[4096,1024]{1,0:T(8,128)(2,1)}) %all-gather.18.cloned.1.call-update) | async-done | bytes 8388624 | tf_op jit(solution)/shard_map/all_gather | solution.py:151
  382.1 27.7 %convert_reduce_fusion = (f32[4096]{0:T(1024)S(1)}, bf16[512,4096]{1,0:T(8,128)(2,1)S(1)}, f32[512,4096]{1,0:T(8,128)}) fusion(f32[512,4096]{1,0:T(8,128)} %fusion.38, f32[4096]{0:T(1024)S(1)} %add.283, bf16[512,1024]{1,0:T(8,128)(2,1)S(1)} %copy-done.17, bf16[4096,1024]{1,0:T(8,128)(2,1)} %all-gather.18.cloned.1.call-done), kind=kOutput, calls=%fused_computation.13 | convolution fusion | flops 4452249600 | bytes 30441472 | tf_op jit(solution)/shard_map/dot_general | solution.py:71
  423.8 15.4 %fusion.12 = bf16[2,16,64,1024]{3,2,1,0:T(8,128)(2,1)} fusion(bf16[2,256,16,64]{1,3,2,0:T(8,128)(2,1)S(1)} %copy.167, f32[2,16,256,1024]{3,2,1,0:T(8,128)} %get-tuple-element.135, f32[2,16,256]{2,1,0:T(8,128)S(1)} %log_add_fusion), kind=kOutput, calls=%fused_computation.33 | convolution fusion | flops 1092616192 | bytes 38830080 | tf_op jit(solution)/shard_map/rhqk,rqhe->rkhe/dot_general | solution.py:227
  445.5 25.9 %multiply_reduce_fusion = (f32[2,16,256]{2,1,0:T(8,128)S(1)}, f32[2,16,256,1024]{3,2,1,0:T(8,128)}) fusion(f32[2,16,256,1024]{3,2,1,0:T(8,128)} %get-tuple-element.135, f32[2,16,256]{2,1,0:T(8,128)S(1)} %log_add_fusion, bf16[2,256,16,64]{1,3,2,0:T(8,128)(2,1)S(1)} %copy.167, bf16[2,1024,16,64]{1,3,2,0:T(8,128)(2,1)} %bitcast.103), kind=kOutput, calls=%fused_computation.1 | convolution fusion | flops 1098899456 | bytes 72417280 | tf_op jit(solution)/shard_map/rqhe,rkhe->rhqk/dot_general | solution.py:233
  471.4 28.0 %multiply_convert_fusion = bf16[2,16,256,1024]{3,2,1,0:T(8,128)(2,1)} fusion(f32[2,16,256,1024]{3,2,1,0:T(8,128)} %get-tuple-element.140, f32[2,16,256,1024]{3,2,1,0:T(8,128)} %get-tuple-element.135, f32[2,16,256]{2,1,0:T(8,128)S(1)} %get-tuple-element.139, f32[2,16,256]{2,1,0:T(8,128)S(1)} %log_add_fusion), kind=kLoop, calls=%fused_computation | loop fusion | flops 33554432 | bytes 83951616 | tf_op jit(solution)/shard_map/convert_element_type | solution.py:237
  499.5 10.8 multiply_convert_fusion.1
  510.2 6.2 copy.170
  522.8 10.8 convert_reduce_fusion.4
  538.3 20.6 %reduce-scatter.10.cloned.1.call-done = bf16[2,256,1024]{2,1,0:T(8,128)(2,1)} async-done(((bf16[2,1024,1024]{2,1,0:T(8,128)(2,1)}), bf16[2,256,1024]{2,1,0:T(8,128)(2,1)}) %reduce-scatter.10.cloned.1.call-update) | async-done | bytes 1048592 | tf_op jit(solution)/shard_map/reduce_scatter | solution.py:249
  562.6 9.0 multiply_reduce_fusion.2
  572.8 10.1 fusion.20
  583.6 13.3 fusion.37
  597.0 10.0 multiply_convert_fusion.2
  607.0 10.4 fusion.49
  618.1 10.9 multiply_convert_fusion.5
  634.2 63.7 %reduce-scatter.16.cloned.1.call-done = f32[32,1024]{1,0:T(8,128)} async-done(((f32[1024,1024]{1,0:T(8,128)}), f32[32,1024]{1,0:T(8,128)}) %reduce-scatter.16.cloned.1.call-update) | async-done | bytes 131088 | tf_op jit(solution)/shard_map/reduce_scatter | solution.py:297
  699.8 131.1 %reduce-scatter.22.cloned.1.call-done = f32[32,12]{1,0:T(8,128)} async-done(((f32[1024,12]{1,0:T(8,128)}), f32[32,12]{1,0:T(8,128)}) %reduce-scatter.22.cloned.1.call-update) | async-done | bytes 1552
  832.4 161.7 %reduce-scatter.14.cloned.1.call-done = f32[32,3072]{1,0:T(8,128)} async-done(((f32[1024,3072]{1,0:T(8,128)}), f32[32,3072]{1,0:T(8,128)}) %reduce-scatter.14.cloned.1.call-update) | async-done | bytes 393232 | tf_op jit(solution)/shard_map/reduce_scatter | solution.py:296
  996.5 184.7 %reduce-scatter.18.cloned.1.call-done = f32[32,4096]{1,0:T(8,128)} async-done(((f32[1024,4096]{1,0:T(8,128)}), f32[32,4096]{1,0:T(8,128)}) %reduce-scatter.18.cloned.1.call-update) | async-done | bytes 524304 | tf_op jit(solution)/shard_map/reduce_scatter | solution.py:298
  1183.6 185.1 %reduce-scatter.20.cloned.1.call-done = f32[128,1024]{1,0:T(8,128)} async-done(((f32[4096,1024]{1,0:T(8,128)}), f32[128,1024]{1,0:T(8,128)}) %reduce-scatter.20.cloned.1.call-update) | async-done | bytes 524304 | tf_op jit(solution)/shard_map/reduce_scatter | solution.py:299
  1371.3 128.3 %all-reduce.2.cloned.1.call-done = f32[49,1024]{1,0:T(8,128)} async-done(((f32[49,1024]{1,0:T(8,128)}), f32[49,1024]{1,0:T(8,128)}) %all-reduce.2.cloned.1.call-update) | async-done | bytes 200720 | tf_op jit(solution)/shard_map/psum | solution.py:275
  (219 shorter events, 107.8 us)
Async XLA Ops:
  7.2 76.5 %all-gather.8.cloned.1.call-start = ((), (), s32[]{:S(2)}) async-start(), calls=%async_computation.7 | async-start | bytes 6488064 | tf_op jit(solution)/shard_map/all_gather | solution.py:148
  9.0 117.4 %all-gather.12.cloned.1.call-start = ((), (), s32[]{:S(2)}) async-start(), calls=%async_computation.9 | async-start | bytes 5242880 | tf_op jit(solution)/shard_map/all_gather | solution.py:173
  11.4 93.8 %copy-start.28 = (s32[2,1024]{1,0:T(2,128)}, s32[2,1024]{1,0:T(2,128)S(1)}, u32[]{:S(2)}) copy-start(s32[2,1024]{1,0:T(2,128)S(1)} %get-tuple-element.76) | copy-start | bytes 24580
  11.5 95.0 %copy-start.29 = (f32[1,2,2,128]{3,1,2,0:T(2,128)}, f32[1,2,2,128]{3,1,2,0:T(2,128)S(1)}, u32[]{:S(2)}) copy-start(f32[1,2,2,128]{3,1,2,0:T(2,128)S(1)} %copy.183) | copy-start | bytes 6148
  12.0 77.5 %copy-start.21 = (f32[7,8,2,256]{3,1,2,0:T(8,128)}, f32[7,8,2,256]{3,1,2,0:T(8,128)S(1)}, u32[]{:S(2)}) copy-start(f32[7,8,2,256]{3,1,2,0:T(8,128)S(1)} %copy.182) | copy-start | bytes 344068
  59.9 163.0 %copy-start.2 = (f32[512,1024]{1,0:T(8,128)}, f32[512,1024]{1,0:T(8,128)S(1)}, u32[]{:S(2)}) copy-start(f32[512,1024]{1,0:T(8,128)S(1)} %get-tuple-element.133) | copy-start | bytes 6291460
  61.2 241.4 %copy-start.47 = (f32[1024,1]{0,1:T(1,128)}, f32[1024,1]{0,1:T(1,128)S(1)}, u32[]{:S(2)}) copy-start(f32[1024,1]{0,1:T(1,128)S(1)} %get-tuple-element.121) | copy-start | bytes 12292
  93.3 69.8 %all-gather.10.cloned.1.call-start = ((), (), s32[]{:S(2)}) async-start(), calls=%async_computation.8 | async-start | bytes 5242880 | tf_op jit(solution)/shard_map/all_gather | solution.py:174
  97.7 125.2 %all-gather.14.cloned.1.call-start = ((), (), s32[]{:S(2)}) async-start(), calls=%async_computation.10 | async-start | bytes 2162688 | tf_op jit(solution)/shard_map/all_gather | solution.py:149
  98.4 204.2 %all-gather.16.cloned.1.call-start = ((), (), s32[]{:S(2)}) async-start(), calls=%async_computation.11 | async-start | bytes 8650752 | tf_op jit(solution)/shard_map/all_gather | solution.py:150
  100.3 281.8 %all-gather.18.cloned.1.call-start = ((), (), s32[]{:S(2)}) async-start(), calls=%async_computation.12 | async-start | bytes 8650752 | tf_op jit(solution)/shard_map/all_gather | solution.py:151
  102.3 433.8 %reduce-scatter.12.cloned.1.call-start = ((), (), s32[]{:S(2)}) async-start(), calls=%async_computation.14 | async-start | bytes 5242880 | tf_op jit(solution)/shard_map/reduce_scatter | solution.py:252
  302.6 79.5 %copy-start.17 = (bf16[512,1024]{1,0:T(8,128)(2,1)S(1)}, bf16[512,1024]{1,0:T(8,128)(2,1)}, u32[]{:S(2)}) copy-start(bf16[512,1024]{1,0:T(8,128)(2,1)} %fusion.17) | copy-start | bytes 3145732
  314.6 95.2 %copy-start.11 = (f32[512,1024]{1,0:T(8,128)S(1)}, f32[512,1024]{1,0:T(8,128)}, u32[]{:S(2)}) copy-start(f32[512,1024]{1,0:T(8,128)} %copy-done.10) | copy-start | bytes 6291460
  445.5 113.4 %reduce-scatter.10.cloned.1.call-start = ((), (), s32[]{:S(2)}) async-start(), calls=%async_computation.13 | async-start | bytes 5242880 | tf_op jit(solution)/shard_map/reduce_scatter | solution.py:249
  516.5 181.5 %reduce-scatter.16.cloned.1.call-start = ((), (), s32[]{:S(2)}) async-start(), calls=%async_computation.17 | async-start | bytes 4325376 | tf_op jit(solution)/shard_map/reduce_scatter | solution.py:297
  521.1 309.8 %reduce-scatter.22.cloned.1.call-start = ((), (), s32[]{:S(2)}) async-start(), calls=%async_computation.20 | async-start | bytes 540672
  572.7 421.3 %reduce-scatter.14.cloned.1.call-start = ((), (), s32[]{:S(2)}) async-start(), calls=%async_computation.16 | async-start | bytes 12976128 | tf_op jit(solution)/shard_map/reduce_scatter | solution.py:296
  582.9 598.3 %reduce-scatter.18.cloned.1.call-start = ((), (), s32[]{:S(2)}) async-start(), calls=%async_computation.18 | async-start | bytes 17301504 | tf_op jit(solution)/shard_map/reduce_scatter | solution.py:298
  596.9 771.8 %reduce-scatter.20.cloned.1.call-start = ((), (), s32[]{:S(2)}) async-start(), calls=%async_computation.19 | async-start | bytes 17301504 | tf_op jit(solution)/shard_map/reduce_scatter | solution.py:299
  617.4 882.2 %all-reduce.2.cloned.1.call-start = ((), (), s32[]{:S(2)}) async-start(), calls=%async_computation.15 | async-start | bytes 458752 | tf_op jit(solution)/shard_map/psum | solution.py:275
  630.6 201.1 %copy-start.33 = (f32[32,12]{0,1:T(8,128)S(1)}, f32[32,12]{0,1:T(8,128)}, u32[]{:S(2)}) copy-start(f32[32,12]{0,1:T(8,128)} %param.27) | copy-start | bytes 4612
  630.6 201.1 %copy-start.44 = (f32[32,12]{0,1:T(8,128)S(1)}, f32[32,12]{0,1:T(8,128)}, u32[]{:S(2)}) copy-start(f32[32,12]{0,1:T(8,128)} %param.32) | copy-start | bytes 4612
  630.6 201.1 %copy-start.45 = (f32[32,12]{0,1:T(8,128)S(1)}, f32[32,12]{0,1:T(8,128)}, u32[]{:S(2)}) copy-start(f32[32,12]{0,1:T(8,128)} %param.37) | copy-start | bytes 4612
  630.6 363.4 %copy-start.16 = (f32[32,3072]{1,0:T(8,128)S(1)}, f32[32,3072]{1,0:T(8,128)}, u32[]{:S(2)}) copy-start(f32[32,3072]{1,0:T(8,128)} %param.23) | copy-start | bytes 1179652
  632.1 549.1 %copy-start.13 = (f32[32,4096]{1,0:T(8,128)S(1)}, f32[32,4096]{1,0:T(8,128)}, u32[]{:S(2)}) copy-start(f32[32,4096]{1,0:T(8,128)} %param.25) | copy-start | bytes 1572868
  632.1 549.1 %copy-start.23 = (f32[32,4096]{1,0:T(8,128)S(1)}, f32[32,4096]{1,0:T(8,128)}, u32[]{:S(2)}) copy-start(f32[32,4096]{1,0:T(8,128)} %param.30) | copy-start | bytes 1572868
  632.1 549.1 %copy-start.24 = (f32[32,4096]{1,0:T(8,128)S(1)}, f32[32,4096]{1,0:T(8,128)}, u32[]{:S(2)}) copy-start(f32[32,4096]{1,0:T(8,128)} %param.35) | copy-start | bytes 1572868
  634.2 734.5 %copy-start.14 = (f32[128,1024]{1,0:T(8,128)S(1)}, f32[128,1024]{1,0:T(8,128)}, u32[]{:S(2)}) copy-start(f32[128,1024]{1,0:T(8,128)} %param.26) | copy-start | bytes 1572868
  634.2 734.5 %copy-start.25 = (f32[128,1024]{1,0:T(8,128)S(1)}, f32[128,1024]{1,0:T(8,128)}, u32[]{:S(2)}) copy-start(f32[128,1024]{1,0:T(8,128)} %param.31) | copy-start | bytes 1572868
  831.7 539.6 %copy-start.32 = (f32[32,12]{0,1:T(8,128)}, f32[32,12]{0,1:T(8,128)S(1)}, u32[]{:S(2)}) copy-start(f32[32,12]{0,1:T(8,128)S(1)} %copy.177) | copy-start | bytes 4612
  994.1 507.2 %copy-start.1 = (f32[49,1024]{1,0:T(8,128)S(1)}, f32[49,1024]{1,0:T(8,128)}, u32[]{:S(2)}) copy-start(f32[49,1024]{1,0:T(8,128)} %param.22) | copy-start | bytes 602116
  (36 other events, 580.1 us)
Sparse Core Ops, SparseCore 0:
  11.5 72.1 all-gather.7
  93.5 32.9 all-gather.11
  128.6 34.4 all-gather.9
  166.4 56.4 all-gather.13
  226.1 76.4 all-gather.15
  305.9 76.1 all-gather.17
  445.6 42.6 reduce-scatter.11
  516.6 42.2 reduce-scatter.9
  561.8 136.1 reduce-scatter.15
  700.6 130.2 reduce-scatter.21
  838.5 155.4 reduce-scatter.13
  996.8 184.4 reduce-scatter.17
  1184.1 184.5 reduce-scatter.19
  1374.7 124.9 all-reduce.1
where the time goes:
time: 1510 us
  waiting for transfers between devices  1090 us (72%)
  matrix products  212 us (14%)
  other arithmetic  84.6 us (6%)
  local copies, waits for them, and re-layouts  62.6 us (4%)
  blocking collectives  43.8 us (3%)
    reduce_scatter x1, waiting for transfers between devices, per_device(): lax.psum_scatter(grad_down, ('img', 'seq'), scatter_dimension=0, tiled=True)  185 us
    reduce_scatter x1, waiting for transfers between devices, per_device(): lax.psum_scatter(grad_up, ('img', 'seq'), scatter_dimension=0, tiled=True)  185 us
    reduce_scatter x1, waiting for transfers between devices, per_device(): lax.psum_scatter(grad_in_matrix, ('img', 'seq'), scatter_dimension=0, til...  162 us
    unnamed x15, waiting for transfers between devices  131 us
    psum x1, waiting for transfers between devices, per_device(): table_grad = lax.psum(table_part, ('img', 'seq'))  128 us
    all_gather x1, waiting for transfers between devices, per_device(): lax.all_gather(cast_up, ('img', 'seq'), axis=0, tiled=True)  75 us
    all_gather x1, waiting for transfers between devices, per_device(): lax.all_gather(cast_down, ('img', 'seq'), axis=0, tiled=True)  67.4 us
    reduce_scatter x1, waiting for transfers between devices, per_device(): lax.psum_scatter(grad_out_matrix, ('img', 'seq'), scatter_dimension=0, ti...  63.7 us
  transfers between devices with their start and end apart: 14, of which 13 were waited for; matrix products, arithmetic and copies ran while one was open for 18% of the time, Pallas kernels for 0%

commit v1 on v0

--- a/solution.py
+++ b/solution.py
@@ -9,6 +9,16 @@
 PRECISE = lax.Precision.HIGHEST
 FIRST_CORRECTION = 0.9999734386011124
 SECOND_CORRECTION = 0.0952078528862911
+
+
+def collect(x, axis, dim):
+    ways, here, step = (lax.axis_size(axis), lax.axis_index(axis), x.shape[dim])
+    dims = [n * ways if d == dim else n for d, n in enumerate(x.shape)]
+    full = lax.dynamic_update_slice_in_dim(jnp.zeros(dims, x.dtype), x, here * step, axis=dim)
+    for far in range(1, ways):
+        x = lax.ppermute(x, axis, [(d, (d + 1) % ways) for d in range(ways)])
+        full = lax.dynamic_update_slice_in_dim(full, x, (here - far) % ways * step, axis=dim)
+    return full
 
 
 def layout(res_ids, positions):
@@ -171,7 +181,7 @@
     )
     keys_all, values_all = (
         lax.all_gather(key_rows, "seq", axis=1, tiled=True),
-        lax.all_gather(value_rows, "seq", axis=1, tiled=True),
+        collect(value_rows, "seq", 1),
     )
     key_len = keys_all.shape[1]
     query_heads = query.reshape(row_count, local_len, head_count, head_size)

time: 1510 us -> 1490 us (0.987)
  waiting for transfers between devices: 1090 us -> 1040 us
  local copies, waits for them, and re-layouts: 62.6 us -> 78.1 us
    ppermute x0 -> x3, waiting for transfers between devices: none -> 43.6 us  [collect(): x = lax.ppermute(x, axis, [(d, (d + 1) % ways) for d in range(ways)])]
    all_gather x1, waiting for transfers between devices: 75 us -> 36 us  [per_device(): lax.all_gather(cast_up, ('img', 'seq'), axis=0, tiled=True)]
    all_gather x1 -> x0, waiting for transfers between devices: 30.4 us -> none  [per_device(): lax.all_gather(value_rows, 'seq', axis=1, tiled=True)]
    unnamed x15 -> x14, waiting for transfers between devices: 131 us -> 131 us
  transfers between devices with their start and end apart: 14 -> 16, of which waited for: 13 -> 12; matrix products, arithmetic and copies ran while one was open for 18% -> 20% of each run, Pallas kernels for 0% -> 0%
where the time goes in v1:
time: 1490 us; the launch traced here: 1480 us
  waiting for transfers between devices  1040 us (70%)
  matrix products  212 us (14%)
  other arithmetic  82.2 us (6%)
  local copies, waits for them, and re-layouts  78.1 us (5%)
  blocking collectives  43.7 us (3%)
  between operations  15 us (1%)
    reduce_scatter x1, waiting for transfers between devices, per_device(): lax.psum_scatter(grad_down, ('img', 'seq'), scatter_dimension=0, tiled=True)  185 us
    reduce_scatter x1, waiting for transfers between devices, per_device(): lax.psum_scatter(grad_up, ('img', 'seq'), scatter_dimension=0, tiled=True)  185 us
    reduce_scatter x1, waiting for transfers between devices, per_device(): lax.psum_scatter(grad_in_matrix, ('img', 'seq'), scatter_dimension=0, til...  161 us
    unnamed x14, waiting for transfers between devices  131 us
    psum x1, waiting for transfers between devices, per_device(): table_grad = lax.psum(table_part, ('img', 'seq'))  128 us
    all_gather x1, waiting for transfers between devices, per_device(): lax.all_gather(cast_down, ('img', 'seq'), axis=0, tiled=True)  67.4 us
    reduce_scatter x1, waiting for transfers between devices, per_device(): lax.psum_scatter(grad_out_matrix, ('img', 'seq'), scatter_dimension=0, ti...  63.2 us
    all_gather x1, blocking collectives, per_device(): lax.all_gather(cast_vectors, ('img', 'seq'), axis=0, tiled=True)  43.7 us
  transfers between devices with their start and end apart: 16, of which 12 were waited for; matrix products, arithmetic and copies ran while one was open for 20% of the time, Pallas kernels for 0%

profile of v1, /device:TPU:1, one launch (start us, length us, event | category | flops | bytes accessed | tf_op | source)
XLA Modules:
  0.0 1482.9 jit_solution(8546717222389246874)
XLA Ops:
  12.7 43.7 %all-gather = bf16[32,32,12]{1,2,0:T(8,128)(2,1)S(1)} all-gather(bf16[1,32,12]{1,2,0:T(8,128)(2,1)S(1)} %convert_bitcast_fusion), channel_id=1, replica_groups=mesh['img'=8,'seq'=4] {'img','seq'}, dimensions={0}, use_global_device_ids=true | all-gather | bytes 25344 | tf_op jit(solution)/shard_map/all_gather | solution.py:162
  61.2 22.5 %all-gather.7.cloned.1.call-done = bf16[1024,3072]{1,0:T(8,128)(2,1)} async-done(((bf16[32,3072]{1,0:T(8,128)(2,1)}), bf16[1024,3072]{1,0:T(8,128)(2,1)}) %all-gather.7.cloned.1.call-update) | async-done | bytes 6291472 | tf_op jit(solution)/shard_map/all_gather | solution.py:158
  102.0 31.9 %collective-permute-done = bf16[2,256,1024]{2,1,0:T(8,128)(2,1)S(1)} collective-permute-done((bf16[2,256,1024]{2,1,0:T(8,128)(2,1)S(1)}, bf16[2,256,1024]{2,1,0:T(8,128)(2,1)S(1)}, u32[]{:S(2)}, u32[]{:S(2)}) %collective-permute-start) | collective-permute-done | bytes 1048608 | tf_op jit(solution)/shard_map/ppermute | solution.py:19
  137.3 11.7 collective-permute-done.1
  183.6 6.2 copy.183
  189.9 16.1 %fusion.47 = (f32[2,16,256]{2,1,0:T(8,128)S(1)}, f32[2,16,256,1024]{3,2,1,0:T(8,128)}) fusion(bf16[2,256,16,64]{1,3,2,0:T(8,128)(2,1)S(1)} %copy.184, bf16[2,1024,16,64]{1,3,2,0:T(8,128)(2,1)} %bitcast.100, pred[2,256,1024]{2,1,0:T(8,128)(4,1)} %broadcast_compare_fusion), kind=kOutput, calls=%fused_computation.151 | convolution fusion | flops 1098899456 | bytes 39354368 | tf_op jit(solution)/shard_map/rqhe,rkhe->rhqk/dot_general | solution.py:104
  206.0 14.5 fusion
  220.5 15.4 %fusion.19 = bf16[2,256,16,64]{1,3,2,0:T(8,128)(2,1)S(1)} fusion(bf16[2,1024,16,64]{1,3,2,0:T(8,128)(2,1)} %bitcast.6, f32[2,16,256,1024]{3,2,1,0:T(8,128)} %get-tuple-element.135, f32[2,16,256]{2,1,0:T(8,128)S(1)} %fusion, f32[2,16,256]{2,1,0:T(8,128)S(1)} %get-tuple-element.134), kind=kOutput, calls=%fused_computation.62 | convolution fusion | flops 1099431936 | bytes 38862848 | tf_op jit(solution)/shard_map/rhqk,rkhe->rqhe/dot_general | solution.py:197
  242.3 36.0 %all-gather.13.cloned.1.call-done = bf16[1024,4096]{1,0:T(8,128)(2,1)} async-done(((bf16[32,4096]{1,0:T(8,128)(2,1)}), bf16[1024,4096]{1,0:T(8,128)(2,1)}) %all-gather.13.cloned.1.call-update) | async-done | bytes 8388624 | tf_op jit(solution)/shard_map/all_gather | solution.py:160
  278.3 12.0 fusion.39
  290.3 67.4 %all-gather.15.cloned.1.call-done = bf16[4096,1024]{1,0:T(8,128)(2,1)} async-done(((bf16[128,1024]{1,0:T(8,128)(2,1)}), bf16[4096,1024]{1,0:T(8,128)(2,1)}) %all-gather.15.cloned.1.call-update) | async-done | bytes 8388624 | tf_op jit(solution)/shard_map/all_gather | solution.py:161
  357.8 27.7 %convert_reduce_fusion = (f32[4096]{0:T(1024)S(1)}, bf16[512,4096]{1,0:T(8,128)(2,1)S(1)}, f32[512,4096]{1,0:T(8,128)}) fusion(f32[512,4096]{1,0:T(8,128)} %fusion.39, f32[4096]{0:T(1024)S(1)} %add.312, bf16[512,1024]{1,0:T(8,128)(2,1)S(1)} %copy-done.21, bf16[4096,1024]{1,0:T(8,128)(2,1)} %all-gather.15.cloned.1.call-done), kind=kOutput, calls=%fused_computation.13 | convolution fusion | flops 4452249600 | bytes 30441472 | tf_op jit(solution)/shard_map/dot_general | solution.py:81
  399.5 15.4 %fusion.12 = bf16[2,16,64,1024]{3,2,1,0:T(8,128)(2,1)} fusion(bf16[2,256,16,64]{1,3,2,0:T(8,128)(2,1)S(1)} %copy.188, f32[2,16,256,1024]{3,2,1,0:T(8,128)} %get-tuple-element.135, f32[2,16,256]{2,1,0:T(8,128)S(1)} %log_add_fusion), kind=kOutput, calls=%fused_computation.33 | convolution fusion | flops 1092616192 | bytes 38830080 | tf_op jit(solution)/shard_map/rhqk,rqhe->rkhe/dot_general | solution.py:237
  414.9 6.2 copy.193
  421.2 25.9 %multiply_reduce_fusion = (f32[2,16,256]{2,1,0:T(8,128)S(1)}, f32[2,16,256,1024]{3,2,1,0:T(8,128)}) fusion(f32[2,16,256,1024]{3,2,1,0:T(8,128)} %get-tuple-element.135, f32[2,16,256]{2,1,0:T(8,128)S(1)} %log_add_fusion, bf16[2,256,16,64]{1,3,2,0:T(8,128)(2,1)S(1)} %copy.188, bf16[2,1024,16,64]{1,3,2,0:T(8,128)(2,1)} %bitcast.6), kind=kOutput, calls=%fused_computation.1 | convolution fusion | flops 1098899456 | bytes 72417280 | tf_op jit(solution)/shard_map/rqhe,rkhe->rhqk/dot_general | solution.py:243
  447.0 28.1 %multiply_convert_fusion = bf16[2,16,256,1024]{3,2,1,0:T(8,128)(2,1)} fusion(f32[2,16,256,1024]{3,2,1,0:T(8,128)} %get-tuple-element.140, f32[2,16,256,1024]{3,2,1,0:T(8,128)} %get-tuple-element.135, f32[2,16,256]{2,1,0:T(8,128)S(1)} %get-tuple-element.139, f32[2,16,256]{2,1,0:T(8,128)S(1)} %log_add_fusion), kind=kLoop, calls=%fused_computation | loop fusion | flops 33554432 | bytes 83951616 | tf_op jit(solution)/shard_map/convert_element_type | solution.py:247
  475.1 10.8 multiply_convert_fusion.1
  485.9 6.2 copy.191
  498.4 10.8 convert_reduce_fusion.4
  514.0 20.6 %reduce-scatter.10.cloned.1.call-done = bf16[2,256,1024]{2,1,0:T(8,128)(2,1)} async-done(((bf16[2,1024,1024]{2,1,0:T(8,128)(2,1)}), bf16[2,256,1024]{2,1,0:T(8,128)(2,1)}) %reduce-scatter.10.cloned.1.call-update) | async-done | bytes 1048592 | tf_op jit(solution)/shard_map/reduce_scatter | solution.py:259
  538.3 9.0 multiply_reduce_fusion.2
  548.5 10.1 fusion.20
  559.2 13.3 fusion.38
  572.7 10.0 multiply_convert_fusion.2
  582.6 10.4 fusion.50
  593.7 10.9 multiply_convert_fusion.5
  609.9 63.2 %reduce-scatter.16.cloned.1.call-done = f32[32,1024]{1,0:T(8,128)} async-done(((f32[1024,1024]{1,0:T(8,128)}), f32[32,1024]{1,0:T(8,128)}) %reduce-scatter.16.cloned.1.call-update) | async-done | bytes 131088 | tf_op jit(solution)/shard_map/reduce_scatter | solution.py:307
  674.9 131.2 %reduce-scatter.22.cloned.1.call-done = f32[32,12]{1,0:T(8,128)} async-done(((f32[1024,12]{1,0:T(8,128)}), f32[32,12]{1,0:T(8,128)}) %reduce-scatter.22.cloned.1.call-update) | async-done | bytes 1552
  807.5 161.3 %reduce-scatter.14.cloned.1.call-done = f32[32,3072]{1,0:T(8,128)} async-done(((f32[1024,3072]{1,0:T(8,128)}), f32[32,3072]{1,0:T(8,128)}) %reduce-scatter.14.cloned.1.call-update) | async-done | bytes 393232 | tf_op jit(solution)/shard_map/reduce_scatter | solution.py:306
  971.3 184.8 %reduce-scatter.18.cloned.1.call-done = f32[32,4096]{1,0:T(8,128)} async-done(((f32[1024,4096]{1,0:T(8,128)}), f32[32,4096]{1,0:T(8,128)}) %reduce-scatter.18.cloned.1.call-update) | async-done | bytes 524304 | tf_op jit(solution)/shard_map/reduce_scatter | solution.py:308
  1158.5 184.9 %reduce-scatter.20.cloned.1.call-done = f32[128,1024]{1,0:T(8,128)} async-done(((f32[4096,1024]{1,0:T(8,128)}), f32[128,1024]{1,0:T(8,128)}) %reduce-scatter.20.cloned.1.call-update) | async-done | bytes 524304 | tf_op jit(solution)/shard_map/reduce_scatter | solution.py:309
  1346.0 128.4 %all-reduce.2.cloned.1.call-done = f32[49,1024]{1,0:T(8,128)} async-done(((f32[49,1024]{1,0:T(8,128)}), f32[49,1024]{1,0:T(8,128)}) %all-reduce.2.cloned.1.call-update) | async-done | bytes 200720 | tf_op jit(solution)/shard_map/psum | solution.py:285
  (240 shorter events, 121.3 us)
Async XLA Ops:
  7.2 76.5 %all-gather.7.cloned.1.call-start = ((), (), s32[]{:S(2)}) async-start(), calls=%async_computation.7 | async-start | bytes 6488064 | tf_op jit(solution)/shard_map/all_gather | solution.py:158
  9.0 174.6 %all-gather.9.cloned.1.call-start = ((), (), s32[]{:S(2)}) async-start(), calls=%async_computation.8 | async-start | bytes 5242880 | tf_op jit(solution)/shard_map/all_gather | solution.py:183
  11.4 140.8 %copy-start.33 = (s32[2,1024]{1,0:T(2,128)}, s32[2,1024]{1,0:T(2,128)S(1)}, u32[]{:S(2)}) copy-start(s32[2,1024]{1,0:T(2,128)S(1)} %get-tuple-element.76) | copy-start | bytes 24580
  11.5 144.3 %copy-start.34 = (f32[1,2,2,128]{3,1,2,0:T(2,128)}, f32[1,2,2,128]{3,1,2,0:T(2,128)S(1)}, u32[]{:S(2)}) copy-start(f32[1,2,2,128]{3,1,2,0:T(2,128)S(1)} %copy.204) | copy-start | bytes 6148
  59.9 177.4 %copy-start.2 = (f32[512,1024]{1,0:T(8,128)}, f32[512,1024]{1,0:T(8,128)S(1)}, u32[]{:S(2)}) copy-start(f32[512,1024]{1,0:T(8,128)S(1)} %get-tuple-element.133) | copy-start | bytes 6291460
  61.2 217.1 %copy-start.52 = (f32[1024,1]{0,1:T(1,128)}, f32[1024,1]{0,1:T(1,128)S(1)}, u32[]{:S(2)}) copy-start(f32[1024,1]{0,1:T(1,128)S(1)} %get-tuple-element.121) | copy-start | bytes 12292
  93.5 143.8 %all-gather.11.cloned.1.call-start = ((), (), s32[]{:S(2)}) async-start(), calls=%async_computation.9 | async-start | bytes 2162688 | tf_op jit(solution)/shard_map/all_gather | solution.py:159
  94.2 184.1 %all-gather.13.cloned.1.call-start = ((), (), s32[]{:S(2)}) async-start(), calls=%async_computation.10 | async-start | bytes 8650752 | tf_op jit(solution)/shard_map/all_gather | solution.py:160
  95.0 262.7 %all-gather.15.cloned.1.call-start = ((), (), s32[]{:S(2)}) async-start(), calls=%async_computation.11 | async-start | bytes 8650752 | tf_op jit(solution)/shard_map/all_gather | solution.py:161
  95.8 415.9 %reduce-scatter.12.cloned.1.call-start = ((), (), s32[]{:S(2)}) async-start(), calls=%async_computation.13 | async-start | bytes 5242880 | tf_op jit(solution)/shard_map/reduce_scatter | solution.py:262
  100.8 33.1 %collective-permute-start = (bf16[2,256,1024]{2,1,0:T(8,128)(2,1)S(1)}, bf16[2,256,1024]{2,1,0:T(8,128)(2,1)S(1)}, u32[]{:S(2)}, u32[]{:S(2)}) collective-permute-start(bf16[2,256,1024]{2,1,0:T(8,128)(2,1)S(1)} %bitcast.109), channel_id=1, source_target_pairs={{0,1},{1,2},{2,3},{3,0},{4,5},{5,6},{6,7},{7,4},{8,9},{9,10},{10,1... | collective-permute-start | bytes 3145736 | tf_op jit(solution)/shard_map/ppermute | solution.py:19
  134.9 14.2 collective-permute-start.1
  149.1 29.9 %collective-permute-start.2 = (bf16[2,256,1024]{2,1,0:T(8,128)(2,1)}, bf16[2,256,1024]{2,1,0:T(8,128)(2,1)}, u32[]{:S(2)}, u32[]{:S(2)}) collective-permute-start(bf16[2,256,1024]{2,1,0:T(8,128)(2,1)} %collective-permute-done.1), channel_id=1, source_target_pairs={{0,1},{1,2},{2,3},{3,0},{4,5},{5,6},{6,7},{7,4},{8,9},{9,10},{10,1... | collective-permute-start | bytes 3145736 | tf_op jit(solution)/shard_map/ppermute | solution.py:19
  290.3 95.1 %copy-start.11 = (f32[512,1024]{1,0:T(8,128)S(1)}, f32[512,1024]{1,0:T(8,128)}, u32[]{:S(2)}) copy-start(f32[512,1024]{1,0:T(8,128)} %copy-done.10) | copy-start | bytes 6291460
  421.1 113.4 %reduce-scatter.10.cloned.1.call-start = ((), (), s32[]{:S(2)}) async-start(), calls=%async_computation.12 | async-start | bytes 5242880 | tf_op jit(solution)/shard_map/reduce_scatter | solution.py:259
  492.1 180.9 %reduce-scatter.16.cloned.1.call-start = ((), (), s32[]{:S(2)}) async-start(), calls=%async_computation.16 | async-start | bytes 4325376 | tf_op jit(solution)/shard_map/reduce_scatter | solution.py:307
  496.7 309.4 %reduce-scatter.22.cloned.1.call-start = ((), (), s32[]{:S(2)}) async-start(), calls=%async_computation.19 | async-start | bytes 540672
  548.4 420.4 %reduce-scatter.14.cloned.1.call-start = ((), (), s32[]{:S(2)}) async-start(), calls=%async_computation.15 | async-start | bytes 12976128 | tf_op jit(solution)/shard_map/reduce_scatter | solution.py:306
  558.6 597.5 %reduce-scatter.18.cloned.1.call-start = ((), (), s32[]{:S(2)}) async-start(), calls=%async_computation.17 | async-start | bytes 17301504 | tf_op jit(solution)/shard_map/reduce_scatter | solution.py:308
  572.6 770.8 %reduce-scatter.20.cloned.1.call-start = ((), (), s32[]{:S(2)}) async-start(), calls=%async_computation.18 | async-start | bytes 17301504 | tf_op jit(solution)/shard_map/reduce_scatter | solution.py:309
  593.0 881.4 %all-reduce.2.cloned.1.call-start = ((), (), s32[]{:S(2)}) async-start(), calls=%async_computation.14 | async-start | bytes 458752 | tf_op jit(solution)/shard_map/psum | solution.py:285
  606.2 200.7 %copy-start.38 = (f32[32,12]{0,1:T(8,128)S(1)}, f32[32,12]{0,1:T(8,128)}, u32[]{:S(2)}) copy-start(f32[32,12]{0,1:T(8,128)} %param.27) | copy-start | bytes 4612
  606.2 200.7 %copy-start.49 = (f32[32,12]{0,1:T(8,128)S(1)}, f32[32,12]{0,1:T(8,128)}, u32[]{:S(2)}) copy-start(f32[32,12]{0,1:T(8,128)} %param.32) | copy-start | bytes 4612
  606.2 200.7 %copy-start.50 = (f32[32,12]{0,1:T(8,128)S(1)}, f32[32,12]{0,1:T(8,128)}, u32[]{:S(2)}) copy-start(f32[32,12]{0,1:T(8,128)} %param.37) | copy-start | bytes 4612
  606.2 362.6 %copy-start.20 = (f32[32,3072]{1,0:T(8,128)S(1)}, f32[32,3072]{1,0:T(8,128)}, u32[]{:S(2)}) copy-start(f32[32,3072]{1,0:T(8,128)} %param.23) | copy-start | bytes 1179652
  607.8 548.3 %copy-start.16 = (f32[32,4096]{1,0:T(8,128)S(1)}, f32[32,4096]{1,0:T(8,128)}, u32[]{:S(2)}) copy-start(f32[32,4096]{1,0:T(8,128)} %param.25) | copy-start | bytes 1572868
  607.8 548.3 %copy-start.28 = (f32[32,4096]{1,0:T(8,128)S(1)}, f32[32,4096]{1,0:T(8,128)}, u32[]{:S(2)}) copy-start(f32[32,4096]{1,0:T(8,128)} %param.30) | copy-start | bytes 1572868
  607.8 548.3 %copy-start.29 = (f32[32,4096]{1,0:T(8,128)S(1)}, f32[32,4096]{1,0:T(8,128)}, u32[]{:S(2)}) copy-start(f32[32,4096]{1,0:T(8,128)} %param.35) | copy-start | bytes 1572868
  609.8 733.6 %copy-start.18 = (f32[128,1024]{1,0:T(8,128)S(1)}, f32[128,1024]{1,0:T(8,128)}, u32[]{:S(2)}) copy-start(f32[128,1024]{1,0:T(8,128)} %param.26) | copy-start | bytes 1572868
  609.8 733.6 %copy-start.30 = (f32[128,1024]{1,0:T(8,128)S(1)}, f32[128,1024]{1,0:T(8,128)}, u32[]{:S(2)}) copy-start(f32[128,1024]{1,0:T(8,128)} %param.31) | copy-start | bytes 1572868
  806.9 539.1 %copy-start.37 = (f32[32,12]{0,1:T(8,128)}, f32[32,12]{0,1:T(8,128)S(1)}, u32[]{:S(2)}) copy-start(f32[32,12]{0,1:T(8,128)S(1)} %copy.198) | copy-start | bytes 4612
  968.8 507.2 %copy-start.1 = (f32[49,1024]{1,0:T(8,128)S(1)}, f32[49,1024]{1,0:T(8,128)}, u32[]{:S(2)}) copy-start(f32[49,1024]{1,0:T(8,128)} %param.22) | copy-start | bytes 602116
  (43 other events, 764.1 us)
Sparse Core Ops, SparseCore 0:
  11.5 72.1 all-gather.6
  93.6 43.7 all-gather.8
  140.8 57.6 all-gather.10
  201.8 76.4 all-gather.12
  281.6 76.1 all-gather.14
  421.2 42.6 reduce-scatter.11
  492.2 42.2 reduce-scatter.9
  537.4 135.5 reduce-scatter.15
  675.9 130.1 reduce-scatter.21
  813.6 155.2 reduce-scatter.13
  971.7 184.3 reduce-scatter.17
  1158.8 184.5 reduce-scatter.19
  1349.5 124.8 all-reduce.1
